TPU v7x, 32 devices: a whole 2x2x4 slice. The times are simulated.
32 devices in a mesh: dp: 4 (over y, x), ctx: 4 (over z), tensor: 2 (over core).
Axes of the slice: x: 2, y: 2, z: 4, core: 2. Of those that a mesh axis runs over, the one named last changes fastest.
Arguments:
- hidden: bfloat16 [4, 1024, 1024], P('dp', 'ctx'), may hold values from -6 to 6
- segment_ids: int32 [4, 1024], P('dp', 'ctx'), may hold values from 0 to 5, as said below
- cotangent: bfloat16 [4, 1024, 1024], P('dp', 'ctx'), may hold values from -6 to 6
- input_gain: float32 [1024], replicated, may hold values from 0.5 to 1.5
- gate_weight: bfloat16 [1024, 2048], P('dp', 'tensor'), may hold values from -0.1875 to 0.1875
- value_weight: bfloat16 [1024, 2048], P('dp', 'tensor'), may hold values from -0.1875 to 0.1875
- state_weight: bfloat16 [1024, 256], P('dp'), may hold values from -0.1875 to 0.1875
- step_weight: bfloat16 [1024, 32], P('dp', 'tensor'), may hold values from -0.1875 to 0.1875
- conv_weight: float32 [4, 2304], replicated, may hold values from -3 to 3
- conv_bias: float32 [2304], replicated, may hold values from -3 to 3
- step_bias: float32 [32], replicated, may hold values from -4 to -1
- decay_log: float32 [32], replicated, may hold values from -6.5 to -1.5
- skip_gain: float32 [32], replicated, may hold values from 0.5 to 1.5
- mixer_gain: float32 [2048], replicated, may hold values from 0.5 to 1.5
- out_weight: bfloat16 [2048, 1024], P('tensor', 'dp'), may hold values from -0.125 to 0.125
Outputs:
- output: bfloat16 [4, 1024, 1024], P('dp', 'ctx')
- grad_hidden: float32 [4, 1024, 1024], P('dp', 'ctx')
- grad_input_gain: float32 [1024], replicated
- grad_gate_weight: float32 [1024, 2048], P('dp', 'tensor')
- grad_value_weight: float32 [1024, 2048], P('dp', 'tensor')
- grad_state_weight: float32 [1024, 256], P('dp')
- grad_step_weight: float32 [1024, 32], P('dp', 'tensor')
- grad_conv_weight: float32 [4, 2304], replicated
- grad_conv_bias: float32 [2304], replicated
- grad_step_bias: float32 [32], replicated
- grad_decay_log: float32 [32], replicated
- grad_skip_gain: float32 [32], replicated
- grad_mixer_gain: float32 [2048], replicated
- grad_out_weight: float32 [2048, 1024], P('tensor', 'dp')
Inputs may be any that keep to these rules, and one draw needn't show every extreme that they name: `segment_ids`: within each sequence the ids start at 0, never fall and rise by one at each new document. Every document has 200 to 512 tokens, except the last one of a sequence, which may be cut short by the sequence's end. The first document of the first sequence has exactly 512 tokens; every document of the last sequence has exactly 200 tokens (the final one possibly cut short).
All inputs are finite; a program needn't handle non-finite values.
Results may differ from a plain program's by a relative error of at most 0.014.
Values may be sent and summed in bfloat16 or wider, within the bound.
A program may use at most 192 MiB of HBM per device.

v0:
```python
from functools import partial
import jax
import jax.numpy as jnp
from jax import lax
from jax.sharding import PartitionSpec as P

GROUP = 128
epsilon = 1e-05
highest = lax.Precision.HIGHEST


def shifted(array, axis, by):
    size = lax.axis_size(axis)
    pairs = [(i, i + by) for i in range(size) if 0 <= i + by < size]
    return lax.ppermute(array, axis, pairs)


def carried_in_2(array, axis, combine, identity):
    size, here = (lax.axis_size(axis), lax.axis_index(axis))
    everything = jax.tree.map(
        lambda part, kind: lax.all_gather(part.astype(kind), axis),
        array,
        (jnp.bfloat16, jnp.bfloat16),
    )
    start = jax.tree.map(
        lambda part, zero: jnp.broadcast_to(jnp.asarray(zero, part.dtype), part.shape),
        array,
        identity,
    )

    def turn(k, before):
        reached = k < here
        new = combine(
            before, jax.tree.map(lambda part, own: part[k].astype(own.dtype), everything, array)
        )
        return jax.tree.map(lambda a, b: jnp.where(reached, a, b), new, before)

    return lax.fori_loop(0, size, turn, start)


def prefix(array, axis, join, neutral):
    count = lax.axis_size(axis)
    place = lax.axis_index(axis)
    ahead = count - 1 - place
    gathered = jax.tree.map(
        lambda a, kind: lax.all_gather(a.astype(kind), axis),
        array,
        jax.tree.map(lambda a: jnp.bfloat16 if a.dtype == jnp.float32 else a.dtype, array),
    )
    state = jax.tree.map(lambda a, e: jnp.zeros_like(a) + jnp.asarray(e, a.dtype), array, neutral)

    def one(turn, state):
        source = count - 1 - turn
        return join(
            state,
            jax.tree.map(
                lambda a, own: lax.dynamic_index_in_dim(a, source, 0, False).astype(own.dtype),
                gathered,
                array,
            ),
        )

    return lax.fori_loop(0, ahead, one, state)


def rms_scale(values, scaling):
    return values * lax.rsqrt(jnp.mean(values * values, axis=-1, keepdims=True) + epsilon) * scaling


def group_step(carry, item, rates):
    values, inputs_b, inputs_c, delta, segments, previous = item
    log_decay = delta * rates[None, :]
    running = jnp.cumsum(log_decay, axis=0)
    length = segments.shape[0]
    order = jnp.arange(length)
    allowed = (segments[:, None] == segments[None, :]) & (order[:, None] >= order[None, :])
    spread = running.T[:, :, None] - running.T[:, None, :]
    decay = jnp.where(allowed[None], jnp.exp(jnp.where(allowed[None], spread, 0.0)), 0.0)
    scores = jnp.dot(inputs_c, inputs_b.T, precision=highest)
    mixing = decay * scores[None] * delta.T[:, None, :]
    inner = jnp.einsum("hts,shp->thp", mixing, values, precision=highest)
    entry = jnp.exp(running) * (segments == previous).astype(jnp.float32)[:, None]
    carried = jnp.einsum("tn,hpn->thp", inputs_c, carry, precision=highest) * entry[:, :, None]
    tail = (
        jnp.exp(running[-1][None, :] - running)
        * (segments == segments[-1]).astype(jnp.float32)[:, None]
        * delta
    )
    fade = jnp.exp(running[-1]) * (segments[-1] == previous).astype(jnp.float32)
    update = jnp.einsum("sh,shp,sn->hpn", tail, values, inputs_b, precision=highest)
    return (carry * fade[:, None, None] + update, inner + carried)


def combine_states(earlier, later):
    return (earlier[0] * later[0], later[0][:, None, None] * earlier[1] + later[1])


def body(
    hidden,
    segment_ids,
    cotangent,
    input_gain,
    gate_weight,
    value_weight,
    state_weight,
    step_weight,
    conv_weight,
    conv_bias,
    step_bias,
    decay_log,
    skip_gain,
    mixer_gain,
    out_weight,
):
    tokens = hidden[0]
    wrapped = segment_ids[0] % 128
    cotangent_rows = cotangent[0]
    length = tokens.shape[0]
    width = tokens.shape[1]
    shard = lax.axis_index("tensor")
    shards = lax.axis_size("tensor")
    full_gate, full_value, full_state, full_step, full_out = (
        lax.all_gather(gate_weight, "dp", axis=0, tiled=True),
        lax.all_gather(value_weight, "dp", axis=0, tiled=True),
        lax.all_gather(state_weight, "dp", axis=0, tiled=True),
        lax.all_gather(step_weight, "dp", axis=0, tiled=True),
        lax.all_gather(out_weight, "dp", axis=1, tiled=True),
    )
    local_width = full_gate.shape[1]
    local_heads = full_step.shape[1]
    head_size = local_width // local_heads
    inner_width = local_width * shards
    states = full_state.shape[1] // 2
    reach = conv_weight.shape[0] - 1
    base = tokens.astype(jnp.float32)
    normed_full, norm_back = jax.vjp(rms_scale, base, input_gain)
    normed = normed_full.astype(jnp.bfloat16)
    gate = jnp.dot(normed, full_gate, preferred_element_type=jnp.float32)
    value_pre = jnp.dot(normed, full_value, preferred_element_type=jnp.float32).astype(jnp.bfloat16)
    state_pre = jnp.dot(normed, full_state, preferred_element_type=jnp.float32).astype(jnp.bfloat16)
    raw_step = jnp.dot(normed, full_step, preferred_element_type=jnp.float32)
    conv_input = jnp.concatenate([value_pre, state_pre], 1)
    edge_rows, edge_ids = shifted(
        (conv_input[length - reach :], wrapped[length - reach :].astype(jnp.bfloat16)), "ctx", 1
    )
    padded = jnp.concatenate([edge_rows, conv_input], 0).astype(jnp.float32)
    padded_ids = jnp.concatenate([edge_ids.astype(jnp.int32), wrapped])
    before = padded_ids[reach - 1]
    kernel = jnp.concatenate(
        [
            lax.dynamic_slice_in_dim(conv_weight, shard * local_width, local_width, 1),
            conv_weight[:, inner_width:],
        ],
        1,
    )
    offset = jnp.concatenate(
        [
            lax.dynamic_slice_in_dim(conv_bias, shard * local_width, local_width, 0),
            conv_bias[inner_width:],
        ],
        0,
    )
    local_bias = lax.dynamic_slice_in_dim(step_bias, shard * local_heads, local_heads, 0)
    local_decay = lax.dynamic_slice_in_dim(decay_log, shard * local_heads, local_heads, 0)
    local_skip = lax.dynamic_slice_in_dim(skip_gain, shard * local_heads, local_heads, 0)
    local_gain = lax.dynamic_slice_in_dim(mixer_gain, shard * local_width, local_width, 0)

    def activate(padded_rows, raw_rows, taps, shift_bias, bias_heads):
        total = jnp.broadcast_to(shift_bias[None, :], (length, shift_bias.shape[0]))
        for lag in range(reach + 1):
            begin = reach - lag
            same = (padded_ids[begin : begin + length] == wrapped).astype(jnp.float32)
            total = total + taps[lag][None, :] * padded_rows[begin : begin + length] * same[:, None]
        activated = jax.nn.silu(total)
        values = activated[:, :local_width].reshape(length, local_heads, head_size)
        return (
            values,
            activated[:, local_width : local_width + states],
            activated[:, local_width + states :],
            jax.nn.softplus(raw_rows + bias_heads[None, :]),
        )

    (values, inputs_b, inputs_c, delta), activate_back = jax.vjp(
        activate, padded, raw_step, kernel, offset, local_bias
    )

    def block(values_in, map_in, map_out, delta_in, decay_in, skip_in):
        rates = -jnp.exp(decay_in)
        count = length // GROUP
        previous = jnp.concatenate([before[None], wrapped[GROUP - 1 :: GROUP][: count - 1]])
        items = (
            values_in.reshape(count, GROUP, local_heads, head_size),
            map_in.reshape(count, GROUP, states),
            map_out.reshape(count, GROUP, states),
            delta_in.reshape(count, GROUP, local_heads),
            wrapped.reshape(count, GROUP),
            previous,
        )
        final, outputs = lax.scan(
            partial(group_step, rates=rates),
            jnp.zeros((local_heads, head_size, states), jnp.float32),
            items,
        )
        mixed = outputs.reshape(length, local_heads, head_size) + skip_in[None, :, None] * values_in
        through = jnp.exp(jnp.sum(delta_in * rates[None, :], axis=0)) * (
            wrapped[-1] == before
        ).astype(jnp.float32)
        return (mixed, through, final)

    (mixed_own, through, final), block_back = jax.vjp(
        block, values, inputs_b, inputs_c, delta, local_decay, local_skip
    )
    carried_in = carried_in_2(
        (through, final), "ctx", combine_states, (jnp.ones_like(through), jnp.zeros_like(final))
    )
    entering = carried_in[1]

    def enter(map_out, delta_in, decay_in, state_in):
        running = jnp.cumsum(delta_in * (-jnp.exp(decay_in))[None, :], axis=0)
        scaling = jnp.exp(running) * (wrapped == before).astype(jnp.float32)[:, None]
        return jnp.einsum("tn,hpn->thp", map_out, state_in, precision=highest) * scaling[:, :, None]

    added, enter_back = jax.vjp(enter, inputs_c, delta, local_decay, entering)
    mixed = (mixed_own + added).reshape(length, local_width)
    silu_gate = jax.nn.silu(gate)
    product = mixed * silu_gate
    squares = lax.psum(jnp.sum(product * product, axis=1), "tensor")
    scale = lax.rsqrt(squares / inner_width + epsilon)
    unit = product * scale[:, None]
    gated = (unit * local_gain[None, :]).astype(jnp.bfloat16)
    branch_out = jnp.dot(gated, full_out, preferred_element_type=jnp.float32)
    summed = lax.psum(branch_out.astype(jnp.bfloat16), "tensor").astype(jnp.float32)
    result = (base + summed).astype(jnp.bfloat16)
    grad_gated = jnp.dot(cotangent_rows, full_out.T, preferred_element_type=jnp.float32)
    grad_out = jnp.dot(gated.T, cotangent_rows, preferred_element_type=jnp.float32)
    grad_mgain = jnp.sum(grad_gated * unit, axis=0)
    grad_unit = grad_gated * local_gain[None, :]
    project = lax.psum(jnp.sum(grad_unit * unit, axis=1), "tensor")
    grad_product = scale[:, None] * (grad_unit - unit * (project / inner_width)[:, None])
    grad_mixed = (grad_product * silu_gate).reshape(length, local_heads, head_size)
    sigma = jax.nn.sigmoid(gate)
    grad_gate = grad_product * mixed * sigma * (1.0 + gate * (1.0 - sigma))
    map_one, delta_one, decay_one, grad_entering = enter_back(grad_mixed)
    carried_out = prefix(
        (through, grad_entering),
        "ctx",
        combine_states,
        (jnp.ones_like(through), jnp.zeros_like(grad_entering)),
    )
    grad_final = carried_out[1]
    grad_through = jnp.sum(grad_final * entering, axis=(1, 2))
    grad_values, grad_map_in, map_two, delta_two, decay_two, grad_skip = block_back(
        (grad_mixed, grad_through, grad_final)
    )
    grad_padded, grad_raw, grad_kernel, grad_offset, grad_bias = activate_back(
        (grad_values, grad_map_in, map_one + map_two, delta_one + delta_two)
    )
    edge_grad = shifted(grad_padded[:reach], "ctx", -1)
    grad_input = grad_padded[reach:].at[length - reach :].add(edge_grad)
    low_gate = grad_gate.astype(jnp.bfloat16)
    low_input = grad_input.astype(jnp.bfloat16)
    low_step = grad_raw.astype(jnp.bfloat16)
    normed_part = (
        jnp.dot(low_gate, full_gate.T, preferred_element_type=jnp.float32)
        + jnp.dot(low_input[:, :local_width], full_value.T, preferred_element_type=jnp.float32)
        + jnp.dot(low_input[:, local_width:], full_state.T, preferred_element_type=jnp.float32)
        + jnp.dot(low_step, full_step.T, preferred_element_type=jnp.float32)
    )
    grad_normed = lax.psum(normed_part.astype(jnp.bfloat16), "tensor").astype(jnp.float32)
    grad_base, grad_gain = norm_back(grad_normed)
    grad_tokens = cotangent_rows.astype(jnp.float32) + grad_base
    grad_gate_w = jnp.dot(normed.T, low_gate, preferred_element_type=jnp.float32)
    grad_value_w = jnp.dot(normed.T, low_input[:, :local_width], preferred_element_type=jnp.float32)
    grad_state_w = jnp.dot(normed.T, low_input[:, local_width:], preferred_element_type=jnp.float32)
    grad_step_w = jnp.dot(normed.T, low_step, preferred_element_type=jnp.float32)
    pieces = (
        lax.psum_scatter(
            grad_gate_w.astype(jnp.bfloat16), "dp", scatter_dimension=0, tiled=True
        ).astype(jnp.float32),
        lax.psum_scatter(
            grad_value_w.astype(jnp.bfloat16), "dp", scatter_dimension=0, tiled=True
        ).astype(jnp.float32),
        lax.psum_scatter(
            grad_step_w.astype(jnp.bfloat16), "dp", scatter_dimension=0, tiled=True
        ).astype(jnp.float32),
        lax.psum_scatter(
            grad_out.astype(jnp.bfloat16), "dp", scatter_dimension=1, tiled=True
        ).astype(jnp.float32),
    )
    sums = (
        lax.psum(pieces[0].astype(jnp.bfloat16), "ctx").astype(jnp.float32),
        lax.psum(pieces[1].astype(jnp.bfloat16), "ctx").astype(jnp.float32),
        lax.psum(pieces[2].astype(jnp.bfloat16), "ctx").astype(jnp.float32),
        lax.psum(pieces[3].astype(jnp.bfloat16), "ctx").astype(jnp.float32),
    )
    halves = width // shards
    keep_half = (jnp.arange(width) // halves == shard).astype(jnp.float32)
    gain_term = grad_gain * keep_half
    kernel_term = jnp.zeros((reach + 1, inner_width + 2 * states), jnp.float32)
    kernel_term = lax.dynamic_update_slice(
        kernel_term, grad_kernel[:, :local_width], (0, shard * local_width)
    )
    kernel_term = kernel_term.at[:, inner_width:].set(grad_kernel[:, local_width:])
    offset_term = jnp.zeros((inner_width + 2 * states,), jnp.float32)
    offset_term = lax.dynamic_update_slice(
        offset_term, grad_offset[:local_width], (shard * local_width,)
    )
    offset_term = offset_term.at[inner_width:].set(grad_offset[local_width:])
    heads_total = local_heads * shards
    bias_term = lax.dynamic_update_slice(
        jnp.zeros((heads_total,), jnp.float32), grad_bias, (shard * local_heads,)
    )
    decay_term = lax.dynamic_update_slice(
        jnp.zeros((heads_total,), jnp.float32), decay_one + decay_two, (shard * local_heads,)
    )
    skip_term = lax.dynamic_update_slice(
        jnp.zeros((heads_total,), jnp.float32), grad_skip, (shard * local_heads,)
    )
    mgain_term = lax.dynamic_update_slice(
        jnp.zeros((inner_width,), jnp.float32), grad_mgain, (shard * local_width,)
    )
    totals = lax.psum(
        (
            gain_term,
            kernel_term,
            offset_term,
            bias_term,
            decay_term,
            skip_term,
            mgain_term,
            grad_state_w,
        ),
        ("dp", "ctx", "tensor"),
    )
    rows = state_weight.shape[0]
    state_rows = lax.dynamic_slice_in_dim(totals[7], lax.axis_index("dp") * rows, rows, 0)
    return (
        result[None],
        grad_tokens[None],
        totals[0],
        sums[0],
        sums[1],
        state_rows,
        sums[2],
        totals[1],
        totals[2],
        totals[3],
        totals[4],
        totals[5],
        totals[6],
        sums[3],
    )


def solution(mesh):
    in_specs = (
        P("dp", "ctx", None),
        P("dp", "ctx"),
        P("dp", "ctx", None),
        P(),
        P("dp", "tensor"),
        P("dp", "tensor"),
        P("dp", None),
        P("dp", "tensor"),
        P(),
        P(),
        P(),
        P(),
        P(),
        P(),
        P("tensor", "dp"),
    )
    out_specs = (
        P("dp", "ctx", None),
        P("dp", "ctx", None),
        P(),
        P("dp", "tensor"),
        P("dp", "tensor"),
        P("dp", None),
        P("dp", "tensor"),
        P(),
        P(),
        P(),
        P(),
        P(),
        P(),
        P("tensor", "dp"),
    )
    return jax.shard_map(body, mesh=mesh, in_specs=in_specs, out_specs=out_specs, check_vma=False)
```

profile of v0, /device:TPU:0, one launch (start us, length us, event | category | flops | bytes accessed | tf_op | source)
XLA Modules:
  0.0 726.9 jit_solution(9285679522740016677)
XLA Ops:
  8.9 4.9 collective-permute-start
  15.5 8.6 %all_gather.33 = bf16[1024,16]{0,1:T(8,128)(2,1)S(1)} all-gather(bf16[256,16]{0,1:T(8,128)(2,1)} %param.36), channel_id=1, replica_groups=mesh['dp'=4,'ctx'=4,'tensor'=2] {'dp'}, dimensions={0}, use_global_device_ids=true | all-gather | bytes 40960 | tf_op jit(solution)/shard_map/all_gather | solution.py:126
  29.5 13.2 %all_gather.35 = bf16[1024,256]{1,0:T(8,128)(2,1)S(1)} all-gather(bf16[256,256]{1,0:T(8,128)(2,1)S(1)} %copy-done.49), channel_id=1, replica_groups=mesh['dp'=4,'ctx'=4,'tensor'=2] {'dp'}, dimensions={0}, use_global_device_ids=true | all-gather | bytes 655360 | tf_op jit(solution)/shard_map/all_gather | solution.py:125
  67.7 120.8 %while.117 = (s32[]{:T(128)}, f32[16,64,128]{2,1,0:T(8,128)S(1)}, f32[2,128,16,64]{1,0,3,2:T(2,128)}, pred[2,16,128,128]{3,2,1,0:T(32,128)(4,1)}, f32[2,16,128,1...) while((s32[]{:T(128)}, f32[16,64,128]{2,1,0:T(8,128)S(1)}, ...), condition=%wide.region_3.4_spmd.clone, body=%wide.region_1.3_spmd.clone.sunk | while | flops 633275392 | bytes 14210707 | solution.py:199
  88.8 13.1 %dynamic_update_slice.320 = f32[2,128,16,64]{1,0,3,2:T(2,128)} dynamic-update-slice(f32[2,128,16,64]{1,0,3,2:T(2,128)} %get-tuple-element.2790, f32[1,128,16,64]{1,0,3,2:T(1,128)} %bitcast.578, s32[]{:T(128)} %get-tuple-element.2788, s32[]{:T(128)} %constant.380.clone.1..sunk.1, s32[]{:T(128)} %constant.380.clone.1..sunk.1, s32[]{:T(128)} %constant.380.clone.1..sunk.1) | dynamic-update-slice | bytes 1048580 | tf_op jit(solution)/shard_map/jvp()/while/body/jit(dynamic_update_index_in_dim)/dynamic_update_slice | solution.py:199
  149.2 13.1 %dynamic_update_slice.320 = f32[2,128,16,64]{1,0,3,2:T(2,128)} dynamic-update-slice(f32[2,128,16,64]{1,0,3,2:T(2,128)} %get-tuple-element.2790, f32[1,128,16,64]{1,0,3,2:T(1,128)} %bitcast.578, s32[]{:T(128)} %get-tuple-element.2788, s32[]{:T(128)} %constant.380.clone.1..sunk.1, s32[]{:T(128)} %constant.380.clone.1..sunk.1, s32[]{:T(128)} %constant.380.clone.1..sunk.1) | dynamic-update-slice | bytes 1048580 | tf_op jit(solution)/shard_map/jvp()/while/body/jit(dynamic_update_index_in_dim)/dynamic_update_slice | solution.py:199
  195.1 13.5 %all-reduce.13 = bf16[64]{0:T(256)(128)(2,1)S(1)} all-reduce(bf16[64]{0:T(256)(128)(2,1)S(1)} %dynamic-update-slice.8), channel_id=2, replica_groups=mesh['dp'=4,'ctx'=4,'tensor'=2] {'ctx'}, use_global_device_ids=true, to_apply=%add.13 | all-reduce | flops 64 | bytes 256
  211.7 6.7 all-gather.15.cloned.1.call-done
  218.5 4.6 while.118
  229.6 25.3 %all-gather.11.cloned.1.call-done = bf16[1024,1024]{1,0:T(8,128)(2,1)} async-done(((bf16[256,1024]{1,0:T(8,128)(2,1)}), bf16[1024,1024]{1,0:T(8,128)(2,1)}) %all-gather.11.cloned.1.call-update) | async-done | bytes 2097168 | tf_op jit(solution)/shard_map/all_gather | solution.py:123
  261.0 30.6 %all-gather.13.cloned.1.call-done = bf16[1024,1024]{1,0:T(8,128)(2,1)} async-done(((bf16[1024,256]{1,0:T(8,128)(2,1)}), bf16[1024,1024]{1,0:T(8,128)(2,1)}) %all-gather.13.cloned.1.call-update) | async-done | bytes 2097168 | tf_op jit(solution)/shard_map/all_gather | solution.py:127
  291.7 4.0 multiply_reduce_fusion.5
  298.1 4.6 multiply_reduce_fusion.6
  318.0 17.1 %all-gather.17.cloned.1.call-done = bf16[64,64,128]{2,1,0:T(8,128)(2,1)} async-done(((bf16[16,64,128]{2,1,0:T(8,128)(2,1)}), bf16[64,64,128]{2,1,0:T(8,128)(2,1)}) %all-gather.17.cloned.1.call-update) | async-done | bytes 1048592 | tf_op jit(solution)/shard_map/all_gather | solution.py:46
  342.0 62.0 %while.119 = (s32[]{:T(128)}, f32[16]{0:T(128)}, f32[16,64,128]{2,1,0:T(8,128)S(1)}, f32[2,128,16,64]{1,3,2,0:T(8,128)}, f32[2,128,128]{2,1,0:T(8,128)}, /*index...) while((s32[]{:T(128)}, f32[16]{0:T(128)}, ...), condition=%wide.region_26.27_spmd.clone, body=%wide.region_16.26_spmd.clone.sunk | while | flops 1263052800 | bytes 29513872 | solution.py:199
  346.4 4.8 fusion.271
  377.2 4.8 fusion.271
  441.3 16.5 %reduce-scatter.7.cloned.1.call-done = bf16[256,1024]{1,0:T(8,128)(2,1)} async-done(((bf16[1024,1024]{1,0:T(8,128)(2,1)}), bf16[256,1024]{1,0:T(8,128)(2,1)}) %reduce-scatter.7.cloned.1.call-update) | async-done | bytes 524304 | tf_op jit(solution)/shard_map/reduce_scatter | solution.py:280
  458.6 25.4 %reduce-scatter.9.cloned.1.call-done = bf16[256,16]{0,1:T(8,128)(2,1)} async-done(((bf16[1024,16]{0,1:T(8,128)(2,1)}), bf16[256,16]{0,1:T(8,128)(2,1)}) %reduce-scatter.9.cloned.1.call-update) | async-done | bytes 8208 | tf_op jit(solution)/shard_map/reduce_scatter | solution.py:283
  484.0 11.9 %psum.120 = bf16[256,16]{0,1:T(8,128)(2,1)S(1)} all-reduce(bf16[256,16]{0,1:T(8,128)(2,1)} %reduce-scatter.9.cloned.1.call-done), channel_id=1, replica_groups=mesh['dp'=4,'ctx'=4,'tensor'=2] {'ctx'}, use_global_device_ids=true, to_apply=%region_41.42 | all-reduce | flops 4096 | bytes 16384 | tf_op jit(solution)/shard_map/psum | solution.py:293
  496.5 123.7 %all-reduce.21.cloned.1.call-done = f32[1024,256]{1,0:T(8,128)} async-done(((f32[1024,256]{1,0:T(8,128)}), f32[1024,256]{1,0:T(8,128)}) %all-reduce.21.cloned.1.call-update) | async-done | bytes 1048592 | tf_op jit(solution)/shard_map/psum | solution.py:322
  621.9 19.8 %all-reduce.25.cloned.1.call-done = (bf16[256,1024]{1,0:T(8,128)(2,1)}, bf16[256,1024]{1,0:T(8,128)(2,1)}) async-done(((bf16[256,1024]{1,0:T(8,128)(2,1)}, bf16[256,1024]{1,0:T(8,128)(2,1)}), (bf16[256,1024]{1,0:T(8,128)(2,1)}, bf16[256,1024]{1,0:T(8,128)(2,1)})) %all-reduce.25.cloned.1.call-update) | async-done | bytes 1048592 | tf_op jit(solution)/shard_map/psum | solution.py:232
  643.3 44.3 %all-reduce.14 = (f32[1024]{0:T(1024)}, f32[4,2304]{1,0:T(4,128)}, f32[2304]{0:T(1024)}, f32[32]{0:T(128)}, f32[32]{0:T(128)}, /*index=5*/f32[32]{0:T(128)}, f32[2048]{0:T(1024)}) all-reduce(f32[1024]{0:T(1024)S(1)} %fusion.168, ...), channel_id=1, replica_groups=mesh['dp'=4,'ctx'=4,'tensor'=2] {'dp','ctx','tensor'}, use_global_device_ids=true, to_apply=%region_34.35 | all-reduce | flops 14688 | bytes 117504 | tf_op jit(solution)/shard_map/psum | solution.py:322
  689.2 26.2 %all-reduce.23.cloned.1.call-done = (bf16[256,1024]{1,0:T(8,128)(2,1)}, bf16[256,1024]{1,0:T(8,128)(2,1)}, bf16[1024,256]{1,0:T(8,128)(2,1)}) async-done(((bf16[256,1024]{1,0:T(8,128)(2,1)}, bf16[256,1024]{1,0:T(8,128)(2,1)}, bf16[1024,256]{1,0:T(8,128)(2,1)}), (bf16[256,1024]{1,0:T(8,128)(2,1)}, bf16[256,1024]{1,0:T(8,128)(2,1)}, bf16[1024,256]{1,0:T(8,128)(2,1)})) %all-reduce.23.cloned.1.call-update) | async-done | bytes 1572880 | tf_op jit(solution)/shard_map/psum | solution.py:291
  (607 shorter events, 277.4 us)
Async XLA Ops:
  7.2 42.0 %all-gather.9.cloned.1.call-start = ((), (), s32[]{:S(2)}) async-start(), calls=%async_computation.4 | async-start | bytes 2621440 | tf_op jit(solution)/shard_map/all_gather | solution.py:124
  8.0 210.5 %all-gather.15.cloned.1.call-start = ((), (), s32[]{:S(2)}) async-start(), calls=%async_computation.12 | async-start | bytes 1310720 | tf_op jit(solution)/shard_map/all_gather | solution.py:21
  8.9 35.6 %collective-permute-start = (bf16[3]{0:T(256)(128)(2,1)S(1)}, bf16[3]{0:T(256)(128)(2,1)S(1)}, u32[]{:S(2)}, u32[]{:S(2)}) collective-permute-start(bf16[3]{0:T(256)(128)(2,1)S(1)} %slice.175), channel_id=1, source_target_pairs={{0,2},{2,4},{4,6},{1,3},{3,5},{5,7},{8,10},{10,12},{12,14},{9,11},... | collective-permute-start | bytes 26 | tf_op jit(solution)/shard_map/ppermute | solution.py:15
  51.6 4.8 collective-permute-start.1
  189.3 65.6 %all-gather.11.cloned.1.call-start = ((), (), s32[]{:S(2)}) async-start(), calls=%async_computation.5 | async-start | bytes 2621440 | tf_op jit(solution)/shard_map/all_gather | solution.py:123
  190.1 101.6 %all-gather.13.cloned.1.call-start = ((), (), s32[]{:S(2)}) async-start(), calls=%async_computation.6 | async-start | bytes 2621440 | tf_op jit(solution)/shard_map/all_gather | solution.py:127
  190.7 144.4 %all-gather.17.cloned.1.call-start = ((), (), s32[]{:S(2)}) async-start(), calls=%async_computation.13 | async-start | bytes 1310720 | tf_op jit(solution)/shard_map/all_gather | solution.py:46
  193.5 113.5 %copy-start.47 = (f32[1024]{0:T(1024)}, f32[1024]{0:T(1024)S(1)}, u32[]{:S(2)}) copy-start(f32[1024]{0:T(1024)S(1)} %dynamic_slice.377) | copy-start | bytes 12292
  208.7 95.3 %copy-start.42 = (f32[256,16]{0,1:T(8,128)}, f32[256,16]{0,1:T(8,128)S(1)}, u32[]{:S(2)}) copy-start(f32[256,16]{0,1:T(8,128)S(1)} %fusion.149) | copy-start | bytes 49156
  229.6 62.1 %copy-start.23 = (bf16[1,256,1024]{2,1,0:T(8,128)(2,1)S(1)}, bf16[1,256,1024]{2,1,0:T(8,128)(2,1)}, u32[]{:S(2)}) copy-start(bf16[1,256,1024]{2,1,0:T(8,128)(2,1)} %param.31) | copy-start | bytes 1572868
  258.6 37.1 %copy-start.13 = (f32[256,1024]{1,0:T(8,128)}, f32[256,1024]{1,0:T(8,128)S(1)}, u32[]{:S(2)}) copy-start(f32[256,1024]{1,0:T(8,128)S(1)} %get-tuple-element.2171) | copy-start | bytes 3145732
  261.0 46.0 %copy-start.70 = (f32[256]{0:T(256)}, f32[256]{0:T(256)S(1)}, u32[]{:S(2)}) copy-start(f32[256]{0:T(256)S(1)} %add_rsqrt_fusion) | copy-start | bytes 3076
  306.9 134.4 %reduce-scatter.11.cloned.1.call-start = ((), (), s32[]{:S(2)}) async-start(), calls=%async_computation.11 | async-start | bytes 2621440 | tf_op jit(solution)/shard_map/reduce_scatter | solution.py:286
  310.5 130.8 %reduce-scatter.5.cloned.1.call-start = ((), (), s32[]{:S(2)}) async-start(), calls=%async_computation.7 | async-start | bytes 2621440 | tf_op jit(solution)/shard_map/reduce_scatter | solution.py:277
  317.9 139.9 %reduce-scatter.7.cloned.1.call-start = ((), (), s32[]{:S(2)}) async-start(), calls=%async_computation.8 | async-start | bytes 2621440 | tf_op jit(solution)/shard_map/reduce_scatter | solution.py:280
  416.1 5.7 collective-permute-start.2
  424.3 59.7 %reduce-scatter.9.cloned.1.call-start = ((), (), s32[]{:S(2)}) async-start(), calls=%async_computation.10 | async-start | bytes 40960 | tf_op jit(solution)/shard_map/reduce_scatter | solution.py:283
  434.4 185.8 %all-reduce.21.cloned.1.call-start = ((), (), s32[]{:S(2)}) async-start(), calls=%async_computation.9 | async-start | bytes 2097152 | tf_op jit(solution)/shard_map/psum | solution.py:322
  435.9 205.8 %all-reduce.25.cloned.1.call-start = ((), (), s32[]{:S(2)}) async-start(), calls=%async_computation.15 | async-start | bytes 2097152 | tf_op jit(solution)/shard_map/psum | solution.py:232
  440.3 275.1 %all-reduce.23.cloned.1.call-start = ((), (), s32[]{:S(2)}) async-start(), calls=%async_computation.14 | async-start | bytes 3145728 | tf_op jit(solution)/shard_map/psum | solution.py:291
  457.8 229.8 %copy-start.91 = (f32[256]{0:T(256)S(1)}, f32[256]{0:T(256)}, u32[]{:S(2)}) copy-start(f32[256]{0:T(256)} %copy-done.90) | copy-start | bytes 3076
  457.8 229.8 %copy-start.24 = (bf16[1,256,1024]{2,1,0:T(8,128)(2,1)S(1)}, bf16[1,256,1024]{2,1,0:T(8,128)(2,1)}, u32[]{:S(2)}) copy-start(bf16[1,256,1024]{2,1,0:T(8,128)(2,1)} %param.31) | copy-start | bytes 1572868
  641.7 46.0 %copy-start.29 = (bf16[256,1024]{1,0:T(8,128)(2,1)S(1)}, bf16[256,1024]{1,0:T(8,128)(2,1)}, u32[]{:S(2)}) copy-start(bf16[256,1024]{1,0:T(8,128)(2,1)} %get-tuple-element.2155) | copy-start | bytes 1572868
  641.7 46.0 %copy-start.39 = (bf16[256,1024]{1,0:T(8,128)(2,1)S(1)}, bf16[256,1024]{1,0:T(8,128)(2,1)}, u32[]{:S(2)}) copy-start(bf16[256,1024]{1,0:T(8,128)(2,1)} %get-tuple-element.2154) | copy-start | bytes 1572868
  (124 other events, 902.1 us)
Sparse Core Ops, SparseCore 0:
  9.9 39.2 all-gather.8
  189.5 28.9 all-gather.14
  220.3 34.5 all-gather.10
  256.6 35.0 all-gather.12
  307.0 27.9 all-gather.16
  337.9 34.5 reduce-scatter.10
  375.5 35.2 reduce-scatter.4
  424.4 33.3 reduce-scatter.6
  461.1 22.8 reduce-scatter.8
  489.6 130.5 all-reduce.20
  623.2 18.4 all-reduce.24
  644.1 71.3 all-reduce.22
where the time goes:
time: 741 us; the launch traced here: 727 us
  waiting for transfers between devices  300 us (40%)
  local copies, waits for them, and re-layouts  132 us (18%)
  blocking collectives  96.4 us (13%)
  other arithmetic  85.2 us (11%)
  matrix products  82.3 us (11%)
  between operations  17.8 us (2%)
  starting transfers between devices  10.1 us (1%)
    psum x1, waiting for transfers between devices, body(): lax.psum((gain_term, kernel_term, offset_term, bias_term, decay_term, ski...  124 us
    dynamic_update_slice x32, local copies, waits for them, and re-layouts, block(): lax.scan(partial(group_step, rates=rates), jnp.zeros((local_heads, head_s...  60.8 us
    psum x1, blocking collectives, body(): lax.psum((gain_term, kernel_term, offset_term, bias_term, decay_term, ski...  44.3 us
    all_gather x1, waiting for transfers between devices, body(): lax.all_gather(out_weight, 'dp', axis=1, tiled=True)  30.6 us
    psum x1, waiting for transfers between devices, body(): lax.psum(pieces[0].astype(jnp.bfloat16), 'ctx').astype(jnp.float32)  26.2 us
    reduce_scatter x1, waiting for transfers between devices, body(): lax.psum_scatter(grad_step_w.astype(jnp.bfloat16), 'dp', scatter_dimensio...  25.4 us
    all_gather x1, waiting for transfers between devices, body(): lax.all_gather(gate_weight, 'dp', axis=0, tiled=True)  25.3 us
    psum x1, waiting for transfers between devices, body(): lax.psum(branch_out.astype(jnp.bfloat16), 'tensor').astype(jnp.float32)  19.8 us
  transfers between devices with their start and end apart: 15, of which 12 were waited for; matrix products, arithmetic and copies ran while one was open for 20% of the time, Pallas kernels for 0%

commit v1 on v0

--- a/solution.py
+++ b/solution.py
@@ -320,17 +320,20 @@
         jnp.zeros((inner_width,), jnp.float32), grad_mgain, (shard * local_width,)
     )
     totals = lax.psum(
-        (
-            gain_term,
-            kernel_term,
-            offset_term,
-            bias_term,
-            decay_term,
-            skip_term,
-            mgain_term,
-            grad_state_w,
+        lax.psum(
+            (
+                gain_term,
+                kernel_term,
+                offset_term,
+                bias_term,
+                decay_term,
+                skip_term,
+                mgain_term,
+                grad_state_w,
+            ),
+            ("ctx", "tensor"),
         ),
-        ("dp", "ctx", "tensor"),
+        "dp",
     )
     rows = state_weight.shape[0]
     state_rows = lax.dynamic_slice_in_dim(totals[7], lax.axis_index("dp") * rows, rows, 0)

time: 741 us -> 795 us (1.073)
  waiting for transfers between devices: 300 us -> 352 us
    psum x1, waiting for transfers between devices: 124 us -> 33.6 us  [body(): lax.psum((gain_term, kernel_term, offset_term, bias_term, decay_term, ski...]
    psum x1, waiting for transfers between devices: 26.2 us -> 70 us  [body(): lax.psum(pieces[0].astype(jnp.bfloat16), 'ctx').astype(jnp.float32)]
    reduce_scatter x1, waiting for transfers between devices: 0.02 us -> 38.2 us  [body(): lax.psum_scatter(grad_gate_w.astype(jnp.bfloat16), 'dp', scatter_dimensio...]
    reduce_scatter x1, waiting for transfers between devices: 0.02 us -> 36.3 us  [body(): lax.psum_scatter(grad_out.astype(jnp.bfloat16), 'dp', scatter_dimension=1...]
    reduce_scatter x1, waiting for transfers between devices: 16.5 us -> 38.2 us  [body(): lax.psum_scatter(grad_value_w.astype(jnp.bfloat16), 'dp', scatter_dimensi...]
    psum x0 -> x1, blocking collectives: none -> 18.4 us  [body(): lax.psum(lax.psum((gain_term, kernel_term, offset_term, bias_term, decay_...]
    psum x1, blocking collectives: 44.3 us -> 29.8 us  [body(): lax.psum((gain_term, kernel_term, offset_term, bias_term, decay_term, ski...]
    psum x1, waiting for transfers between devices: 19.8 us -> 9.93 us  [body(): lax.psum(branch_out.astype(jnp.bfloat16), 'tensor').astype(jnp.float32)]
  transfers between devices with their start and end apart: 15 -> 16, of which waited for: 12 -> 15; matrix products, arithmetic and copies ran while one was open for 20% -> 8% of each run, Pallas kernels for 0% -> 0%
where the time goes in v1:
time: 795 us; the launch traced here: 781 us
  waiting for transfers between devices  352 us (44%)
  local copies, waits for them, and re-layouts  129 us (16%)
  blocking collectives  100 us (13%)
  other arithmetic  86.4 us (11%)
  matrix products  81.9 us (10%)
  between operations  17.7 us (2%)
  starting transfers between devices  10.4 us (1%)
    psum x1, waiting for transfers between devices, body(): lax.psum(pieces[0].astype(jnp.bfloat16), 'ctx').astype(jnp.float32)  70 us
    dynamic_update_slice x32, local copies, waits for them, and re-layouts, block(): lax.scan(partial(group_step, rates=rates), jnp.zeros((local_heads, head_s...  61.1 us
    reduce_scatter x1, waiting for transfers between devices, body(): lax.psum_scatter(grad_gate_w.astype(jnp.bfloat16), 'dp', scatter_dimensio...  38.2 us
    reduce_scatter x1, waiting for transfers between devices, body(): lax.psum_scatter(grad_value_w.astype(jnp.bfloat16), 'dp', scatter_dimensi...  38.2 us
    reduce_scatter x1, waiting for transfers between devices, body(): lax.psum_scatter(grad_out.astype(jnp.bfloat16), 'dp', scatter_dimension=1...  36.3 us
    psum x1, waiting for transfers between devices, body(): lax.psum((gain_term, kernel_term, offset_term, bias_term, decay_term, ski...  33.6 us
    all_gather x1, waiting for transfers between devices, body(): lax.all_gather(out_weight, 'dp', axis=1, tiled=True)  30.6 us
    psum x1, blocking collectives, body(): lax.psum((gain_term, kernel_term, offset_term, bias_term, decay_term, ski...  29.8 us
  transfers between devices with their start and end apart: 16, of which 15 were waited for; matrix products, arithmetic and copies ran while one was open for 8% of the time, Pallas kernels for 0%

profile of v1, /device:TPU:0, one launch (start us, length us, event | category | flops | bytes accessed | tf_op | source)
XLA Modules:
  0.0 781.0 jit_solution(5379906702736103072)
XLA Ops:
  8.9 4.9 collective-permute-start
  15.5 8.6 %all_gather.33 = bf16[1024,16]{0,1:T(8,128)(2,1)S(1)} all-gather(bf16[256,16]{0,1:T(8,128)(2,1)} %param.36), channel_id=1, replica_groups=mesh['dp'=4,'ctx'=4,'tensor'=2] {'dp'}, dimensions={0}, use_global_device_ids=true | all-gather | bytes 40960 | tf_op jit(solution)/shard_map/all_gather | solution.py:126
  29.5 13.3 %all_gather.35 = bf16[1024,256]{1,0:T(8,128)(2,1)S(1)} all-gather(bf16[256,256]{1,0:T(8,128)(2,1)S(1)} %copy-done.52), channel_id=1, replica_groups=mesh['dp'=4,'ctx'=4,'tensor'=2] {'dp'}, dimensions={0}, use_global_device_ids=true | all-gather | bytes 655360 | tf_op jit(solution)/shard_map/all_gather | solution.py:125
  67.7 121.3 %while.117 = (s32[]{:T(128)}, f32[16,64,128]{2,1,0:T(8,128)S(1)}, f32[2,128,16,64]{1,0,3,2:T(2,128)}, pred[2,16,128,128]{3,2,1,0:T(32,128)(4,1)}, f32[2,16,128,1...) while((s32[]{:T(128)}, f32[16,64,128]{2,1,0:T(8,128)S(1)}, ...), condition=%wide.region_3.4_spmd.clone, body=%wide.region_1.3_spmd.clone.sunk | while | flops 633275392 | bytes 14210707 | solution.py:199
  88.9 13.1 %dynamic_update_slice.320 = f32[2,128,16,64]{1,0,3,2:T(2,128)} dynamic-update-slice(f32[2,128,16,64]{1,0,3,2:T(2,128)} %get-tuple-element.2797, f32[1,128,16,64]{1,0,3,2:T(1,128)} %bitcast.578, s32[]{:T(128)} %get-tuple-element.2795, s32[]{:T(128)} %constant.380.clone.1..sunk.1, s32[]{:T(128)} %constant.380.clone.1..sunk.1, s32[]{:T(128)} %constant.380.clone.1..sunk.1) | dynamic-update-slice | bytes 1048580 | tf_op jit(solution)/shard_map/jvp()/while/body/jit(dynamic_update_index_in_dim)/dynamic_update_slice | solution.py:199
  149.5 13.1 %dynamic_update_slice.320 = f32[2,128,16,64]{1,0,3,2:T(2,128)} dynamic-update-slice(f32[2,128,16,64]{1,0,3,2:T(2,128)} %get-tuple-element.2797, f32[1,128,16,64]{1,0,3,2:T(1,128)} %bitcast.578, s32[]{:T(128)} %get-tuple-element.2795, s32[]{:T(128)} %constant.380.clone.1..sunk.1, s32[]{:T(128)} %constant.380.clone.1..sunk.1, s32[]{:T(128)} %constant.380.clone.1..sunk.1) | dynamic-update-slice | bytes 1048580 | tf_op jit(solution)/shard_map/jvp()/while/body/jit(dynamic_update_index_in_dim)/dynamic_update_slice | solution.py:199
  195.6 13.5 %all-reduce.13 = bf16[64]{0:T(256)(128)(2,1)S(1)} all-reduce(bf16[64]{0:T(256)(128)(2,1)S(1)} %dynamic-update-slice.8), channel_id=2, replica_groups=mesh['dp'=4,'ctx'=4,'tensor'=2] {'ctx'}, use_global_device_ids=true, to_apply=%add.13 | all-reduce | flops 64 | bytes 256
  212.3 6.7 all-gather.15.cloned.1.call-done
  230.0 25.4 %all-gather.11.cloned.1.call-done = bf16[1024,1024]{1,0:T(8,128)(2,1)} async-done(((bf16[256,1024]{1,0:T(8,128)(2,1)}), bf16[1024,1024]{1,0:T(8,128)(2,1)}) %all-gather.11.cloned.1.call-update) | async-done | bytes 2097168 | tf_op jit(solution)/shard_map/all_gather | solution.py:123
  261.5 30.6 %all-gather.13.cloned.1.call-done = bf16[1024,1024]{1,0:T(8,128)(2,1)} async-done(((bf16[1024,256]{1,0:T(8,128)(2,1)}), bf16[1024,1024]{1,0:T(8,128)(2,1)}) %all-gather.13.cloned.1.call-update) | async-done | bytes 2097168 | tf_op jit(solution)/shard_map/all_gather | solution.py:127
  311.0 23.2 %all-gather.17.cloned.1.call-done = bf16[64,64,128]{2,1,0:T(8,128)(2,1)} async-done(((bf16[16,64,128]{2,1,0:T(8,128)(2,1)}), bf16[64,64,128]{2,1,0:T(8,128)(2,1)}) %all-gather.17.cloned.1.call-update) | async-done | bytes 1048592 | tf_op jit(solution)/shard_map/all_gather | solution.py:46
  341.0 62.2 %while.119 = (s32[]{:T(128)}, f32[16]{0:T(128)}, f32[16,64,128]{2,1,0:T(8,128)S(1)}, f32[2,128,16,64]{1,3,2,0:T(8,128)}, f32[2,128,128]{2,1,0:T(8,128)}, /*index...) while((s32[]{:T(128)}, f32[16]{0:T(128)}, ...), condition=%wide.region_26.27_spmd.clone, body=%wide.region_16.26_spmd.clone.sunk | while | flops 1263052800 | bytes 29513872 | solution.py:199
  345.4 4.8 fusion.271
  445.2 33.6 %all-reduce.23.cloned.1.call-done = f32[1024,256]{1,0:T(8,128)} async-done(((f32[1024,256]{1,0:T(8,128)}), f32[1024,256]{1,0:T(8,128)}) %all-reduce.23.cloned.1.call-update) | async-done | bytes 1048592 | tf_op jit(solution)/shard_map/psum | solution.py:323
  479.7 36.3 %reduce-scatter.11.cloned.1.call-done = bf16[1024,256]{1,0:T(8,128)(2,1)} async-done(((bf16[1024,1024]{1,0:T(8,128)(2,1)}), bf16[1024,256]{1,0:T(8,128)(2,1)}) %reduce-scatter.11.cloned.1.call-update) | async-done | bytes 524304 | tf_op jit(solution)/shard_map/reduce_scatter | solution.py:286
  516.0 38.2 %reduce-scatter.5.cloned.1.call-done = bf16[256,1024]{1,0:T(8,128)(2,1)} async-done(((bf16[1024,1024]{1,0:T(8,128)(2,1)}), bf16[256,1024]{1,0:T(8,128)(2,1)}) %reduce-scatter.5.cloned.1.call-update) | async-done | bytes 524304 | tf_op jit(solution)/shard_map/reduce_scatter | solution.py:277
  554.2 38.2 %reduce-scatter.7.cloned.1.call-done = bf16[256,1024]{1,0:T(8,128)(2,1)} async-done(((bf16[1024,1024]{1,0:T(8,128)(2,1)}), bf16[256,1024]{1,0:T(8,128)(2,1)}) %reduce-scatter.7.cloned.1.call-update) | async-done | bytes 524304 | tf_op jit(solution)/shard_map/reduce_scatter | solution.py:280
  593.2 25.3 %reduce-scatter.9.cloned.1.call-done = bf16[256,16]{0,1:T(8,128)(2,1)} async-done(((bf16[1024,16]{0,1:T(8,128)(2,1)}), bf16[256,16]{0,1:T(8,128)(2,1)}) %reduce-scatter.9.cloned.1.call-update) | async-done | bytes 8208 | tf_op jit(solution)/shard_map/reduce_scatter | solution.py:283
  618.5 12.0 %psum.178 = bf16[256,16]{0,1:T(8,128)(2,1)S(1)} all-reduce(bf16[256,16]{0,1:T(8,128)(2,1)} %reduce-scatter.9.cloned.1.call-done), channel_id=1, replica_groups=mesh['dp'=4,'ctx'=4,'tensor'=2] {'ctx'}, use_global_device_ids=true, to_apply=%region_43.44 | all-reduce | flops 4096 | bytes 16384 | tf_op jit(solution)/shard_map/psum | solution.py:293
  631.0 9.9 %all-reduce.29.cloned.1.call-done = (bf16[256,1024]{1,0:T(8,128)(2,1)}, bf16[256,1024]{1,0:T(8,128)(2,1)}) async-done(((bf16[256,1024]{1,0:T(8,128)(2,1)}, bf16[256,1024]{1,0:T(8,128)(2,1)}), (bf16[256,1024]{1,0:T(8,128)(2,1)}, bf16[256,1024]{1,0:T(8,128)(2,1)})) %all-reduce.29.cloned.1.call-update) | async-done | bytes 1048592 | tf_op jit(solution)/shard_map/psum | solution.py:232
  642.6 29.8 %all-reduce.14 = (f32[1024]{0:T(1024)S(1)}, f32[4,2304]{1,0:T(4,128)S(1)}, f32[2304]{0:T(1024)S(1)}, f32[32]{0:T(128)S(1)}, f32[32]{0:T(128)S(1)}, /*index=5*/f32[32]{0:T(128)S(1)}, f32[2048]{0:T(1024)S(1)}) all-reduce(f32[1024]{0:T(1024)S(1)} %fusion.168, ...), channel_id=1, replica_groups=mesh['dp'=4,'ctx'=4,'tensor'=2] {'ctx','tensor'}, use_global_device_ids=true, to_apply=%region_34.35 | all-reduce | flops 14688 | bytes 117504 | tf_op jit(solution)/shard_map/psum | solution.py:323
  672.4 18.4 %all-reduce.15 = (f32[1024]{0:T(1024)}, f32[4,2304]{1,0:T(4,128)}, f32[2304]{0:T(1024)}, f32[32]{0:T(128)}, f32[32]{0:T(128)}, /*index=5*/f32[32]{0:T(128)}, f32[2048]{0:T(1024)}) all-reduce(f32[1024]{0:T(1024)S(1)} %get-tuple-element.2144, ...), channel_id=1, replica_groups=mesh['dp'=4,'ctx'=4,'tensor'=2] {'dp'}, use_global_device_ids=true, to_apply=%region_35.36 | all-reduce | flops 14688 | bytes 117504 | tf_op jit(solution)/shard_map/psum | solution.py:322
  692.4 5.6 all-reduce.25.cloned.1.call-done
  699.7 70.0 %all-reduce.27.cloned.1.call-done = (bf16[256,1024]{1,0:T(8,128)(2,1)}, bf16[256,1024]{1,0:T(8,128)(2,1)}, bf16[1024,256]{1,0:T(8,128)(2,1)}) async-done(((bf16[256,1024]{1,0:T(8,128)(2,1)}, bf16[256,1024]{1,0:T(8,128)(2,1)}, bf16[1024,256]{1,0:T(8,128)(2,1)}), (bf16[256,1024]{1,0:T(8,128)(2,1)}, bf16[256,1024]{1,0:T(8,128)(2,1)}, bf16[1024,256]{1,0:T(8,128)(2,1)})) %all-reduce.27.cloned.1.call-update) | async-done | bytes 1572880 | tf_op jit(solution)/shard_map/psum | solution.py:291
  (617 shorter events, 293.7 us)
Async XLA Ops:
  7.2 42.0 %all-gather.9.cloned.1.call-start = ((), (), s32[]{:S(2)}) async-start(), calls=%async_computation.4 | async-start | bytes 2621440 | tf_op jit(solution)/shard_map/all_gather | solution.py:124
  8.0 211.0 %all-gather.15.cloned.1.call-start = ((), (), s32[]{:S(2)}) async-start(), calls=%async_computation.13 | async-start | bytes 1310720 | tf_op jit(solution)/shard_map/all_gather | solution.py:21
  8.9 35.6 %collective-permute-start = (bf16[3]{0:T(256)(128)(2,1)S(1)}, bf16[3]{0:T(256)(128)(2,1)S(1)}, u32[]{:S(2)}, u32[]{:S(2)}) collective-permute-start(bf16[3]{0:T(256)(128)(2,1)S(1)} %slice.175), channel_id=1, source_target_pairs={{0,2},{2,4},{4,6},{1,3},{3,5},{5,7},{8,10},{10,12},{12,14},{9,11},... | collective-permute-start | bytes 26 | tf_op jit(solution)/shard_map/ppermute | solution.py:15
  51.6 4.8 collective-permute-start.1
  189.9 65.5 %all-gather.11.cloned.1.call-start = ((), (), s32[]{:S(2)}) async-start(), calls=%async_computation.5 | async-start | bytes 2621440 | tf_op jit(solution)/shard_map/all_gather | solution.py:123
  190.6 101.6 %all-gather.13.cloned.1.call-start = ((), (), s32[]{:S(2)}) async-start(), calls=%async_computation.6 | async-start | bytes 2621440 | tf_op jit(solution)/shard_map/all_gather | solution.py:127
  191.2 143.0 %all-gather.17.cloned.1.call-start = ((), (), s32[]{:S(2)}) async-start(), calls=%async_computation.14 | async-start | bytes 1310720 | tf_op jit(solution)/shard_map/all_gather | solution.py:46
  194.0 104.6 %copy-start.50 = (f32[1024]{0:T(1024)}, f32[1024]{0:T(1024)S(1)}, u32[]{:S(2)}) copy-start(f32[1024]{0:T(1024)S(1)} %dynamic_slice.377) | copy-start | bytes 12292
  209.3 94.0 %copy-start.46 = (f32[256,16]{0,1:T(8,128)}, f32[256,16]{0,1:T(8,128)S(1)}, u32[]{:S(2)}) copy-start(f32[256,16]{0,1:T(8,128)S(1)} %fusion.149) | copy-start | bytes 49156
  230.0 62.2 %copy-start.26 = (bf16[1,256,1024]{2,1,0:T(8,128)(2,1)S(1)}, bf16[1,256,1024]{2,1,0:T(8,128)(2,1)}, u32[]{:S(2)}) copy-start(bf16[1,256,1024]{2,1,0:T(8,128)(2,1)} %param.31) | copy-start | bytes 1572868
  306.0 172.7 %all-reduce.23.cloned.1.call-start = ((), (), s32[]{:S(2)}) async-start(), calls=%async_computation.9 | async-start | bytes 2097152 | tf_op jit(solution)/shard_map/psum | solution.py:323
  413.7 5.7 collective-permute-start.2
  421.2 94.8 %reduce-scatter.11.cloned.1.call-start = ((), (), s32[]{:S(2)}) async-start(), calls=%async_computation.12 | async-start | bytes 2621440 | tf_op jit(solution)/shard_map/reduce_scatter | solution.py:286
  423.9 130.3 %reduce-scatter.5.cloned.1.call-start = ((), (), s32[]{:S(2)}) async-start(), calls=%async_computation.7 | async-start | bytes 2621440 | tf_op jit(solution)/shard_map/reduce_scatter | solution.py:277
  427.2 165.2 %reduce-scatter.7.cloned.1.call-start = ((), (), s32[]{:S(2)}) async-start(), calls=%async_computation.8 | async-start | bytes 2621440 | tf_op jit(solution)/shard_map/reduce_scatter | solution.py:280
  429.6 188.9 %reduce-scatter.9.cloned.1.call-start = ((), (), s32[]{:S(2)}) async-start(), calls=%async_computation.11 | async-start | bytes 40960 | tf_op jit(solution)/shard_map/reduce_scatter | solution.py:283
  440.5 200.5 %all-reduce.29.cloned.1.call-start = ((), (), s32[]{:S(2)}) async-start(), calls=%async_computation.16 | async-start | bytes 2097152 | tf_op jit(solution)/shard_map/psum | solution.py:232
  445.1 252.9 %all-reduce.25.cloned.1.call-start = ((), (), s32[]{:S(2)}) async-start(), calls=%async_computation.10 | async-start | bytes 2097152 | tf_op jit(solution)/shard_map/psum | solution.py:322
  478.8 114.3 %copy-start.82 = (f32[16]{0:T(128)S(1)}, f32[16]{0:T(128)}, u32[]{:S(2)}) copy-start(f32[16]{0:T(128)} %get-tuple-element.3101) | copy-start | bytes 196
  478.8 290.9 %all-reduce.27.cloned.1.call-start = ((), (), s32[]{:S(2)}) async-start(), calls=%async_computation.15 | async-start | bytes 3145728 | tf_op jit(solution)/shard_map/psum | solution.py:291
  592.4 98.4 %copy-start.94 = (f32[256]{0:T(256)S(1)}, f32[256]{0:T(256)}, u32[]{:S(2)}) copy-start(f32[256]{0:T(256)} %copy-done.93) | copy-start | bytes 3076
  592.4 98.4 %copy-start.28 = (bf16[1,256,1024]{2,1,0:T(8,128)(2,1)S(1)}, bf16[1,256,1024]{2,1,0:T(8,128)(2,1)}, u32[]{:S(2)}) copy-start(bf16[1,256,1024]{2,1,0:T(8,128)(2,1)} %param.31) | copy-start | bytes 1572868
  641.0 49.9 %copy-start.34 = (bf16[256,1024]{1,0:T(8,128)(2,1)S(1)}, bf16[256,1024]{1,0:T(8,128)(2,1)}, u32[]{:S(2)}) copy-start(bf16[256,1024]{1,0:T(8,128)(2,1)} %get-tuple-element.2162) | copy-start | bytes 1572868
  641.0 49.9 %copy-start.43 = (bf16[256,1024]{1,0:T(8,128)(2,1)S(1)}, bf16[256,1024]{1,0:T(8,128)(2,1)}, u32[]{:S(2)}) copy-start(bf16[256,1024]{1,0:T(8,128)(2,1)} %get-tuple-element.2161) | copy-start | bytes 1572868
  (128 other events, 1133.7 us)
Sparse Core Ops, SparseCore 0:
  9.9 39.2 all-gather.8
  190.0 28.9 all-gather.14
  220.8 34.5 all-gather.10
  257.1 35.0 all-gather.12
  306.2 27.9 all-gather.16
  421.3 57.4 all-reduce.22
  481.7 34.2 reduce-scatter.10
  519.0 35.1 reduce-scatter.4
  557.2 35.1 reduce-scatter.6
  595.5 22.8 reduce-scatter.8
  621.4 19.5 all-reduce.28
  643.9 54.0 all-reduce.24
  700.6 69.0 all-reduce.26
